TPU v7x, 128 devices: a whole 4x4x4 slice. The times are simulated.
128 devices in a mesh: dom: 128 (over x, y, z, core).
Axes of the slice: x: 4, y: 4, z: 4, core: 2. Of those that a mesh axis runs over, the one named last changes fastest.
Arguments:
- ham_core: float32 [81920, 1280], P('dom')
- halo_rows: float32 [128, 8, 80, 1280], P('dom'), as said below
- halo_request: int32 [128, 160], P('dom'), may hold values from -1 to 159, as said below
- deriv: float32 [3, 20480, 4, 1280], P(None, 'dom'), may hold values from -15 to 15
- e_low: float32 [1], replicated, may hold values from -8 to -5
- e_high: float32 [1], replicated, may hold values from 4.5 to 7.5
- branches: int32 [5], replicated, may hold values from 0 to 1
Outputs:
- density: float32 [81920, 1280], P('dom')
- forces: float32 [3, 20480], P(None, 'dom')
Inputs may be any that keep to these rules, and one draw needn't show every extreme that they name: Entry halo_request[d, k * 20 + s] is an atom index of the owner of block k of d, or -1 for an empty slot; in each block of 20 the live entries come first and are distinct; in every draw some partition asks 20 atoms of each of its 8 neighbours and is asked 20 atoms by each of them. For c < 640: halo_rows[p, k, r, c] equals ham_core[d * 640 + c, 640 + 4 * 20 * k + r] with d = (p - off_k) mod 128.
All inputs are finite; a program needn't handle non-finite values.
Results may differ from a plain program's by a relative error of at most 0.0003.
Values sent between devices are 32-bit elements; how exact they have to be, the bound alone decides.
A program may use at most 128 MiB of HBM per device.

v0:
```python
import jax
import jax.numpy as jnp
from jax import lax
from jax.sharding import PartitionSpec as P

ORB = 4
ATOM_DEV = 160
NB = 4
ITERS = 5


def passed_along(value, axis, steps):
    count = lax.axis_size(axis)
    pairs = [(source, (source + steps) % count) for source in range(count)]
    return lax.ppermute(value, axis, pairs)


def product(left, right):
    return jnp.dot(left, right, precision=lax.Precision.HIGHEST, preferred_element_type=jnp.float32)


def block_offset(block):
    if block < NB:
        return block + 1
    return NB - 1 - block


def per_device(ham_core, halo_rows, halo_request, deriv, e_low, e_high, branches):
    row_count, order_all = ham_core.shape
    request = halo_request[0]
    slot_count = request.shape[0]
    block_count = 2 * NB
    per_block = slot_count // block_count
    live_halo = jnp.repeat((request >= 0).astype(jnp.float32), ORB)
    live_mask = jnp.concatenate([jnp.ones((row_count,), jnp.float32), live_halo])
    spread = e_high[0] - e_low[0]
    diagonal = jnp.diag(e_high[0] * live_mask)
    outgoing = halo_rows[0]
    core_square = None
    pieces = []
    for block in range(block_count):
        pieces.append(passed_along(outgoing[block], "dom", -block_offset(block)))
    arrived = jnp.stack(pieces, axis=0)
    whole_ham = (
        jnp.concatenate([ham_core, arrived.reshape(-1, order_all)], axis=0)
        * live_mask[:, None]
        * live_mask[None, :]
    )
    symmetric = 0.5 * (whole_ham + whole_ham.T)
    projector = (diagonal - symmetric) / spread
    for number in range(ITERS):
        square = product(projector, projector)
        projector = jnp.where(branches[number] == 1, 2.0 * projector - square, square)
    density = projector[:row_count]
    weighted = jnp.sum(density.reshape(ATOM_DEV, ORB, order_all)[None] * deriv, axis=2)
    pair_force = 2.0 * jnp.sum(weighted.reshape(3, ATOM_DEV, -1, ORB), axis=3)
    own_force = jnp.sum(pair_force, axis=2)
    reaction = -jnp.sum(pair_force, axis=1)
    halo_terms = reaction[:, ATOM_DEV:].reshape(3, block_count, per_block)
    request_block = request.reshape(block_count, per_block)
    selector = (
        request_block[:, :, None] == jnp.arange(ATOM_DEV, dtype=jnp.int32)[None, None, :]
    ).astype(jnp.float32)
    owner_terms = jnp.einsum("ckn,kna->kca", halo_terms, selector, precision=lax.Precision.HIGHEST)
    forces = own_force + reaction[:, :ATOM_DEV]
    for block in range(block_count):
        forces = forces + passed_along(owner_terms[block], "dom", block_offset(block))
    return (density, forces)


def solution(mesh):
    in_specs = (
        P("dom", None),
        P("dom", None, None, None),
        P("dom", None),
        P(None, "dom", None, None),
        P(),
        P(),
        P(),
    )
    out_specs = (P("dom", None), P(None, "dom"))
    return jax.shard_map(
        per_device, mesh=mesh, in_specs=in_specs, out_specs=out_specs, check_vma=False
    )
```

profile of v0, /device:TPU:1, one launch (start us, length us, event | category | flops | bytes accessed | tf_op | source)
XLA Modules:
  0.0 290.7 jit_solution(10260487542575131971)
XLA Ops:
  0.7 3.6 %slice_bitcast_fusion = (f32[80,1280]{1,0:T(8,128)}, f32[80,1280]{1,0:T(8,128)}, f32[80,1280]{1,0:T(8,128)}, f32[80,1280]{1,0:T(8,128)}, f32[80,1280]{1,0:T(8,12...) fusion(f32[1,8,80,1280]{3,2,1,0:T(8,128)} %param.8), kind=kLoop, calls=%fused_computation.29 | loop fusion | bytes 6553600 | tf_op jit(solution)/shard_map/squeeze | solution.py:42
  4.3 1.4 collective-permute-start
  5.7 8.5 %collective-permute-start.1 = (f32[80,1280]{1,0:T(8,128)}, f32[80,1280]{1,0:T(8,128)}, u32[]{:S(2)}, u32[]{:S(2)}) collective-permute-start(f32[80,1280]{1,0:T(8,128)} %get-tuple-element.9), channel_id=1, source_target_pairs={{0,126},{1,127},{2,0},{3,1},{4,2},{5,3},{6,4},{7,5},{8,6},{9,7},{1... | collective-permute-start | bytes 1228808 | tf_op jit(solution)/shard_map/ppermute | solution.py:15
  14.2 0.4 collective-permute-start.2
  14.5 3.0 %collective-permute-start.3 = (f32[80,1280]{1,0:T(8,128)}, f32[80,1280]{1,0:T(8,128)}, u32[]{:S(2)}, u32[]{:S(2)}) collective-permute-start(f32[80,1280]{1,0:T(8,128)} %get-tuple-element.7), channel_id=1, source_target_pairs={{0,124},{1,125},{2,126},{3,127},{4,0},{5,1},{6,2},{7,3},{8,4},{9,5... | collective-permute-start | bytes 1228808 | tf_op jit(solution)/shard_map/ppermute | solution.py:15
  17.5 0.0 collective-permute-start.4
  18.2 0.1 broadcast_in_dim.25
  18.2 0.1 reshape.51
  18.4 3.5 %copy.16 = f32[640,1280]{0,1:T(8,128)S(1)} copy(f32[640,1280]{1,0:T(8,128)} %param.7) | data formatting | bytes 6553600 | tf_op args[0]
  22.5 0.7 fusion.23
  26.3 0.5 broadcast.20
  26.9 0.7 reduce.3
  27.5 0.1 eq.60
  27.6 0.0 collective-permute-done
  27.6 0.1 collective-permute-start.5
  27.7 1.8 bitcast_dynamic-update-slice_fusion.7
  29.5 0.0 collective-permute-done.1
  29.5 2.6 collective-permute-start.6
  32.1 1.8 bitcast_dynamic-update-slice_fusion.6
  33.9 9.8 %collective-permute-done.2 = f32[80,1280]{1,0:T(8,128)} collective-permute-done((f32[80,1280]{1,0:T(8,128)}, f32[80,1280]{1,0:T(8,128)}, u32[]{:S(2)}, u32[]{:S(2)}) %collective-permute-start.2) | collective-permute-done | bytes 409632 | tf_op jit(solution)/shard_map/ppermute | solution.py:15
  43.7 10.6 %collective-permute-start.7 = (f32[80,1280]{1,0:T(8,128)}, f32[80,1280]{1,0:T(8,128)S(1)}, u32[]{:S(2)}, u32[]{:S(2)}) collective-permute-start(f32[80,1280]{1,0:T(8,128)} %get-tuple-element.4), channel_id=1, source_target_pairs={{0,4},{1,5},{2,6},{3,7},{4,8},{5,9},{6,10},{7,11},{8,12},{9,13},{1... | collective-permute-start | bytes 1228808 | tf_op jit(solution)/shard_map/ppermute | solution.py:15
  54.2 1.8 bitcast_dynamic-update-slice_fusion.5
  56.0 0.0 collective-permute-done.3
  56.0 1.8 bitcast_dynamic-update-slice_fusion.4
  57.8 0.0 collective-permute-done.4
  57.8 1.8 bitcast_dynamic-update-slice_fusion.3
  59.6 0.8 bitcast_dynamic-update-slice_fusion.2
  60.4 2.4 collective-permute-done.6
  62.8 0.8 bitcast_dynamic-update-slice_fusion.1
  63.5 8.5 %collective-permute-done.7 = f32[80,1280]{1,0:T(8,128)S(1)} collective-permute-done((f32[80,1280]{1,0:T(8,128)}, f32[80,1280]{1,0:T(8,128)S(1)}, u32[]{:S(2)}, u32[]{:S(2)}) %collective-permute-start.7) | collective-permute-done | bytes 409632 | tf_op jit(solution)/shard_map/ppermute | solution.py:15
  72.1 0.8 bitcast_dynamic-update-slice_fusion
  72.8 4.6 %copy.17 = f32[640,1280]{0,1:T(8,128)} copy(f32[640,1280]{1,0:T(8,128)} %bitcast.23) | data formatting | bytes 6553600 | tf_op jit(solution)/shard_map/reshape | solution.py:45
  77.4 4.6 %fusion = f32[1280,1280]{0,1:T(8,128)} fusion(f32[640,1280]{0,1:T(8,128)} %copy.17, f32[640,1280]{0,1:T(8,128)S(1)} %copy.16, f32[1280]{0:T(1024)S(1)} %get-tuple-element.21), kind=kLoop, calls=%fused_computation.6 | loop fusion | flops 4915200 | bytes 13112320 | tf_op jit(solution)/shard_map/mul | solution.py:45
  82.0 8.2 %copy.18 = f32[1280,1280]{1,0:T(8,128)} copy(f32[1280,1280]{0,1:T(8,128)} %fusion) | data formatting | bytes 13107200 | tf_op jit(solution)/shard_map/mul | solution.py:45
  90.2 41.7 %subtract_select_fusion.3 = f32[1280,1280]{1,0:T(8,128)S(1)} fusion(f32[1280,1280]{1,0:T(8,128)} %copy.18, f32[1280,1280]{0,1:T(8,128)} %fusion, f32[]{:T(128)S(6)} %sub.22, f32[1280]{0:T(1024)S(1)} %get-tuple-element.20, pred[]{:T(512)} %bitcast.4), kind=kOutput, calls=%fused_computation.4 | convolution fusion | flops 25190400000 | bytes 19665924 | tf_op jit(solution)/shard_map/dot_general | solution.py:19
  131.8 27.6 %subtract_select_fusion.2 = f32[1280,1280]{1,0:T(8,128)S(1)} fusion(f32[1280,1280]{1,0:T(8,128)S(1)} %subtract_select_fusion.3, pred[]{:T(512)} %bitcast.3), kind=kOutput, calls=%fused_computation.3 | convolution fusion | flops 25170739200 | bytes 13107201 | tf_op jit(solution)/shard_map/dot_general | solution.py:19
  159.4 27.1 %subtract_select_fusion.1 = f32[1280,1280]{1,0:T(8,128)S(1)} fusion(f32[1280,1280]{1,0:T(8,128)S(1)} %subtract_select_fusion.2, pred[]{:T(512)} %bitcast.2), kind=kOutput, calls=%fused_computation.2 | convolution fusion | flops 25170739200 | bytes 13107201 | tf_op jit(solution)/shard_map/dot_general | solution.py:19
  186.5 27.0 %subtract_select_fusion = f32[1280,1280]{1,0:T(8,128)S(1)} fusion(f32[1280,1280]{1,0:T(8,128)S(1)} %subtract_select_fusion.1, pred[]{:T(512)} %bitcast.1), kind=kOutput, calls=%fused_computation.1 | convolution fusion | flops 25170739200 | bytes 13107201 | tf_op jit(solution)/shard_map/dot_general | solution.py:19
  213.5 26.5 %fusion.24 = f32[1280,1280]{1,0:T(8,128)S(1)} fusion(f32[1280,1280]{1,0:T(8,128)S(1)} %subtract_select_fusion), kind=kOutput, calls=%fused_computation.63 | convolution fusion | flops 25165824000 | bytes 13107200 | tf_op jit(solution)/shard_map/dot_general | solution.py:19
  240.1 0.4 subtract_select_fusion.4
  240.5 0.0 copy-start
  240.5 2.7 mul.72
  243.2 10.8 %multiply_reduce_fusion = f32[3,160,1280]{2,1,0:T(8,128)} fusion(f32[3,160,4,1280]{3,2,1,0:T(4,128)} %param.10, f32[160,4,1280]{2,1,0:T(4,128)} %mul.72), kind=kLoop, calls=%fused_computation | loop fusion | flops 4300800 | bytes 15564800 | tf_op jit(solution)/shard_map/reduce_sum | solution.py:55
  254.0 4.8 %copy.19 = f32[3,160,1280]{1,2,0:T(8,128)} copy(f32[3,160,1280]{2,1,0:T(8,128)} %multiply_reduce_fusion) | data formatting | bytes 4915200 | tf_op jit(solution)/shard_map/reduce_sum | solution.py:55
  258.8 5.1 %reshape.53 = f32[3,160,320,4]{1,3,2,0:T(4,128)} reshape(f32[3,160,1280]{1,2,0:T(8,128)} %copy.19) | data formatting | bytes 4915200 | tf_op jit(solution)/shard_map/reshape | solution.py:56
  263.9 4.5 %reduce_sum.37 = f32[3,160,320]{1,2,0:T(8,128)S(1)} reduce(f32[3,160,320,4]{1,3,2,0:T(4,128)} %reshape.53, f32[]{:T(128)} %constant.17.clone.1), dimensions={3}, to_apply=%region_1.2 | reduce | flops 460800 | bytes 3072004 | tf_op jit(solution)/shard_map/reduce_sum | solution.py:56
  268.4 0.3 multiply_reduce_fusion.2
  268.7 0.1 slice.107
  268.8 0.1 reshape.54
  268.8 0.3 fusion.10
  269.1 0.1 collective-permute-start.10
  269.2 0.3 collective-permute-start.11
  269.5 0.5 collective-permute-start.12
  270.0 6.4 %collective-permute-start.13 = (f32[3,160]{1,0:T(4,128)S(1)}, f32[3,160]{1,0:T(4,128)S(1)}, u32[]{:S(2)}, u32[]{:S(2)}) collective-permute-start(f32[3,160]{1,0:T(4,128)S(1)} %get-tuple-element.15), channel_id=1, source_target_pairs={{0,126},{1,127},{2,0},{3,1},{4,2},{5,3},{6,4},{7,5},{8,6},{9,7},{1... | collective-permute-start | bytes 5768 | tf_op jit(solution)/shard_map/ppermute | solution.py:15
  276.5 1.4 collective-permute-start.14
  277.9 0.1 collective-permute-done.10
  277.9 2.6 collective-permute-start.15
  280.5 1.5 collective-permute-start.8
  282.0 0.3 collective-permute-start.9
  282.3 0.0 collective-permute-done.13
  282.3 0.0 collective-permute-done.14
  282.4 0.4 collective-permute-done.8
  282.7 7.1 %collective-permute-done.9 = f32[3,160]{1,0:T(4,128)S(1)} collective-permute-done((f32[3,160]{1,0:T(4,128)S(1)}, f32[3,160]{1,0:T(4,128)S(1)}, u32[]{:S(2)}, u32[]{:S(2)}) %collective-permute-start.9) | collective-permute-done | bytes 1952 | tf_op jit(solution)/shard_map/ppermute | solution.py:15
  289.9 0.6 fusion.20
  (13 shorter events, 0.0 us)
Async XLA Ops:
  0.6 17.5 %copy-start.2 = (s32[1,160]{1,0:T(1,128)S(1)}, s32[1,160]{1,0:T(1,128)}, u32[]{:S(2)}) copy-start(s32[1,160]{1,0:T(1,128)} %param.9) | copy-start | bytes 1924
  0.6 21.8 %copy-start.1 = (s32[5]{0:T(128)S(1)}, s32[5]{0:T(128)}, u32[]{:S(2)}) copy-start(s32[5]{0:T(128)} %param.13) | copy-start | bytes 64
  4.3 23.4 %collective-permute-start = (f32[80,1280]{1,0:T(8,128)}, f32[80,1280]{1,0:T(8,128)}, u32[]{:S(2)}, u32[]{:S(2)}) collective-permute-start(f32[80,1280]{1,0:T(8,128)} %get-tuple-element.10), channel_id=1, source_target_pairs={{0,127},{1,0},{2,1},{3,2},{4,3},{5,4},{6,5},{7,6},{8,7},{9,8},{10,... | collective-permute-start | bytes 1228808 | tf_op jit(solution)/shard_map/ppermute | solution.py:15
  5.7 23.8 %collective-permute-start.1 = (f32[80,1280]{1,0:T(8,128)}, f32[80,1280]{1,0:T(8,128)}, u32[]{:S(2)}, u32[]{:S(2)}) collective-permute-start(f32[80,1280]{1,0:T(8,128)} %get-tuple-element.9), channel_id=1, source_target_pairs={{0,126},{1,127},{2,0},{3,1},{4,2},{5,3},{6,4},{7,5},{8,6},{9,7},{1... | collective-permute-start | bytes 1228808 | tf_op jit(solution)/shard_map/ppermute | solution.py:15
  14.2 29.5 %collective-permute-start.2 = (f32[80,1280]{1,0:T(8,128)}, f32[80,1280]{1,0:T(8,128)}, u32[]{:S(2)}, u32[]{:S(2)}) collective-permute-start(f32[80,1280]{1,0:T(8,128)} %get-tuple-element.8), channel_id=1, source_target_pairs={{0,125},{1,126},{2,127},{3,0},{4,1},{5,2},{6,3},{7,4},{8,5},{9,6},... | collective-permute-start | bytes 1228808 | tf_op jit(solution)/shard_map/ppermute | solution.py:15
  14.5 41.5 %collective-permute-start.3 = (f32[80,1280]{1,0:T(8,128)}, f32[80,1280]{1,0:T(8,128)}, u32[]{:S(2)}, u32[]{:S(2)}) collective-permute-start(f32[80,1280]{1,0:T(8,128)} %get-tuple-element.7), channel_id=1, source_target_pairs={{0,124},{1,125},{2,126},{3,127},{4,0},{5,1},{6,2},{7,3},{8,4},{9,5... | collective-permute-start | bytes 1228808 | tf_op jit(solution)/shard_map/ppermute | solution.py:15
  17.5 40.3 %collective-permute-start.4 = (f32[80,1280]{1,0:T(8,128)}, f32[80,1280]{1,0:T(8,128)}, u32[]{:S(2)}, u32[]{:S(2)}) collective-permute-start(f32[80,1280]{1,0:T(8,128)} %get-tuple-element.6), channel_id=1, source_target_pairs={{0,1},{1,2},{2,3},{3,4},{4,5},{5,6},{6,7},{7,8},{8,9},{9,10},{10,1... | collective-permute-start | bytes 1228808 | tf_op jit(solution)/shard_map/ppermute | solution.py:15
  27.6 32.0 %collective-permute-start.5 = (f32[80,1280]{1,0:T(8,128)}, f32[80,1280]{1,0:T(8,128)S(1)}, u32[]{:S(2)}, u32[]{:S(2)}) collective-permute-start(f32[80,1280]{1,0:T(8,128)} %get-tuple-element.5), channel_id=1, source_target_pairs={{0,2},{1,3},{2,4},{3,5},{4,6},{5,7},{6,8},{7,9},{8,10},{9,11},{10,... | collective-permute-start | bytes 1228808 | tf_op jit(solution)/shard_map/ppermute | solution.py:15
  29.5 33.3 %collective-permute-start.6 = (f32[80,1280]{1,0:T(8,128)}, f32[80,1280]{1,0:T(8,128)S(1)}, u32[]{:S(2)}, u32[]{:S(2)}) collective-permute-start(f32[80,1280]{1,0:T(8,128)} %get-tuple-element.11), channel_id=1, source_target_pairs={{0,3},{1,4},{2,5},{3,6},{4,7},{5,8},{6,9},{7,10},{8,11},{9,12},{10... | collective-permute-start | bytes 1228808 | tf_op jit(solution)/shard_map/ppermute | solution.py:15
  43.7 28.4 %collective-permute-start.7 = (f32[80,1280]{1,0:T(8,128)}, f32[80,1280]{1,0:T(8,128)S(1)}, u32[]{:S(2)}, u32[]{:S(2)}) collective-permute-start(f32[80,1280]{1,0:T(8,128)} %get-tuple-element.4), channel_id=1, source_target_pairs={{0,4},{1,5},{2,6},{3,7},{4,8},{5,9},{6,10},{7,11},{8,12},{9,13},{1... | collective-permute-start | bytes 1228808 | tf_op jit(solution)/shard_map/ppermute | solution.py:15
  240.5 13.5 %copy-start = (f32[640,1280]{1,0:T(8,128)}, f32[640,1280]{1,0:T(8,128)S(1)}, u32[]{:S(2)}) copy-start(f32[640,1280]{1,0:T(8,128)S(1)} %subtract_select_fusion.4) | copy-start | bytes 9830404
  269.1 8.8 %collective-permute-start.10 = (f32[3,160]{1,0:T(4,128)S(1)}, f32[3,160]{1,0:T(4,128)S(1)}, u32[]{:S(2)}, u32[]{:S(2)}) collective-permute-start(f32[3,160]{1,0:T(4,128)S(1)} %get-tuple-element.18), channel_id=1, source_target_pairs={{0,3},{1,4},{2,5},{3,6},{4,7},{5,8},{6,9},{7,10},{8,11},{9,12},{10... | collective-permute-start | bytes 5768 | tf_op jit(solution)/shard_map/ppermute | solution.py:15
  269.2 11.3 %collective-permute-start.11 = (f32[3,160]{1,0:T(4,128)S(1)}, f32[3,160]{1,0:T(4,128)S(1)}, u32[]{:S(2)}, u32[]{:S(2)}) collective-permute-start(f32[3,160]{1,0:T(4,128)S(1)} %get-tuple-element.17), channel_id=1, source_target_pairs={{0,4},{1,5},{2,6},{3,7},{4,8},{5,9},{6,10},{7,11},{8,12},{9,13},{1... | collective-permute-start | bytes 5768 | tf_op jit(solution)/shard_map/ppermute | solution.py:15
  269.5 12.5 %collective-permute-start.12 = (f32[3,160]{1,0:T(4,128)S(1)}, f32[3,160]{1,0:T(4,128)S(1)}, u32[]{:S(2)}, u32[]{:S(2)}) collective-permute-start(f32[3,160]{1,0:T(4,128)S(1)} %get-tuple-element.16), channel_id=1, source_target_pairs={{0,127},{1,0},{2,1},{3,2},{4,3},{5,4},{6,5},{7,6},{8,7},{9,8},{10,... | collective-permute-start | bytes 5768 | tf_op jit(solution)/shard_map/ppermute | solution.py:15
  270.0 12.3 %collective-permute-start.13 = (f32[3,160]{1,0:T(4,128)S(1)}, f32[3,160]{1,0:T(4,128)S(1)}, u32[]{:S(2)}, u32[]{:S(2)}) collective-permute-start(f32[3,160]{1,0:T(4,128)S(1)} %get-tuple-element.15), channel_id=1, source_target_pairs={{0,126},{1,127},{2,0},{3,1},{4,2},{5,3},{6,4},{7,5},{8,6},{9,7},{1... | collective-permute-start | bytes 5768 | tf_op jit(solution)/shard_map/ppermute | solution.py:15
  276.5 5.9 %collective-permute-start.14 = (f32[3,160]{1,0:T(4,128)S(1)}, f32[3,160]{1,0:T(4,128)S(1)}, u32[]{:S(2)}, u32[]{:S(2)}) collective-permute-start(f32[3,160]{1,0:T(4,128)S(1)} %get-tuple-element.14), channel_id=1, source_target_pairs={{0,125},{1,126},{2,127},{3,0},{4,1},{5,2},{6,3},{7,4},{8,5},{9,6},... | collective-permute-start | bytes 5768 | tf_op jit(solution)/shard_map/ppermute | solution.py:15
  277.9 4.4 %collective-permute-start.15 = (f32[3,160]{1,0:T(4,128)S(1)}, f32[3,160]{1,0:T(4,128)S(1)}, u32[]{:S(2)}, u32[]{:S(2)}) collective-permute-start(f32[3,160]{1,0:T(4,128)S(1)} %get-tuple-element.13), channel_id=1, source_target_pairs={{0,124},{1,125},{2,126},{3,127},{4,0},{5,1},{6,2},{7,3},{8,4},{9,5... | collective-permute-start | bytes 5768 | tf_op jit(solution)/shard_map/ppermute | solution.py:15
  280.5 2.2 collective-permute-start.8
  282.0 7.9 %collective-permute-start.9 = (f32[3,160]{1,0:T(4,128)S(1)}, f32[3,160]{1,0:T(4,128)S(1)}, u32[]{:S(2)}, u32[]{:S(2)}) collective-permute-start(f32[3,160]{1,0:T(4,128)S(1)} %get-tuple-element.19), channel_id=1, source_target_pairs={{0,2},{1,3},{2,4},{3,5},{4,6},{5,7},{6,8},{7,9},{8,10},{9,11},{10,... | collective-permute-start | bytes 5768 | tf_op jit(solution)/shard_map/ppermute | solution.py:15
where the time goes:
time: 295 us; the launch traced here: 291 us
  matrix products  150 us (51%)
  local copies, waits for them, and re-layouts  45.2 us (15%)
  starting transfers between devices  39.6 us (13%)
  waiting for transfers between devices  28.3 us (10%)
  other arithmetic  21.9 us (7%)
  between operations  5.55 us (2%)
    dot_general x5, matrix products, product(): jnp.dot(left, right, precision=lax.Precision.HIGHEST, preferred_element_t...  150 us
    ppermute x16, starting transfers between devices, passed_along(): return lax.ppermute(value, axis, pairs)  39.6 us
    ppermute x16, waiting for transfers between devices, passed_along(): return lax.ppermute(value, axis, pairs)  28.3 us
    unnamed x15, local copies, waits for them, and re-layouts  14.5 us
    reduce_sum x1, other arithmetic, per_device(): jnp.sum(density.reshape(ATOM_DEV, ORB, order_all)[None] * deriv, axis=2)  10.8 us
    mul x1, local copies, waits for them, and re-layouts, per_device(): jnp.concatenate([ham_core, arrived.reshape(-1, order_all)], axis=0)  8.17 us
  transfers between devices with their start and end apart: 16, of which 6 were waited for; matrix products, arithmetic and copies ran while one was open for 6% of the time, Pallas kernels for 0%

commit v1 on v0

v1 whole, which is shorter than its diff:
```python
import jax
import jax.numpy as jnp
from jax import lax
from jax.experimental import pallas as pl
from jax.experimental.pallas import tpu as pltpu
from jax.sharding import PartitionSpec as P

ORB = 4
ATOM_DEV = 160
NB = 4
BLOCKS = 2 * NB
ITERS = 5
ROWS = 640
M = 1280
SLOT_ROWS = ROWS // BLOCKS
TILE = 256
COLS = M // TILE
F32 = jnp.float32
BF16 = jnp.bfloat16
MESH = pl.DeviceIdType.MESH


def block_offset(block):
    if block < NB:
        return block + 1
    return NB - 1 - block


def mm(left, right):
    return jnp.dot(left, right, preferred_element_type=F32)


def mm_nt(left, right):
    return lax.dot_general(left, right, (((1,), (1,)), ((), ())), preferred_element_type=F32)


def span(i):
    return slice(i * TILE, (i + 1) * TILE)


def split2(value):
    high = value.astype(BF16)
    return high, (value - high.astype(F32)).astype(BF16)


def split3(value):
    high = value.astype(BF16)
    rest = value - high.astype(F32)
    mid = rest.astype(BF16)
    return high, mid, (rest - mid.astype(F32)).astype(BF16)


def sp2_kernel(
    low_ref, high_ref, branch_ref, request_ref, ham_ref, halo_ref, deriv_ref,
    dens_ref, force_ref,
    core, halo, dbuf, xh, xl, acc, dens, own, select, rsum, fsend, frecv,
    core_sem, deriv_sem, dens_sem, send_sem, recv_sem, fsend_sem, frecv_sem,
):
    count = lax.axis_size("dom")
    me = lax.axis_index("dom")

    def peer(offset):
        return lax.rem(me + offset + count, count)

    load_core = pltpu.make_async_copy(ham_ref, core, core_sem.at[0])
    load_core.start()
    barrier = pltpu.get_barrier_semaphore()
    for k in range(BLOCKS):
        pl.semaphore_signal(barrier, inc=1, device_id=(peer(block_offset(k)),), device_id_type=MESH)
    pl.semaphore_wait(barrier, BLOCKS)
    sends = []
    for k in (3, 7, 2, 6, 1, 5, 0, 4):
        send = pltpu.make_async_remote_copy(
            src_ref=halo_ref.at[0, k, :, ROWS:M],
            dst_ref=halo.at[k * SLOT_ROWS : (k + 1) * SLOT_ROWS],
            send_sem=send_sem.at[k],
            recv_sem=recv_sem.at[k],
            device_id=(peer(-block_offset(k)),),
            device_id_type=MESH,
        )
        send.start()
        sends.append(send)
    load_deriv = []
    for c in range(3):
        for mu in range(ORB):
            load = pltpu.make_async_copy(deriv_ref.at[c, :, mu, :], dbuf.at[c, mu], deriv_sem.at[c * ORB + mu])
            load.start()
            load_deriv.append(load)

    request = request_ref[...]
    live = (request >= 0).astype(F32)
    spread_atom = (
        lax.broadcasted_iota(jnp.int32, (ROWS, ATOM_DEV), 0) // ORB
        == lax.broadcasted_iota(jnp.int32, (ROWS, ATOM_DEV), 1)
    ).astype(F32)
    live_col = jnp.sum(spread_atom * live, axis=1, keepdims=True)
    eight = jnp.broadcast_to(live, (8, ATOM_DEV))
    live_row = mm_nt(eight.astype(BF16), spread_atom.astype(BF16))[0:1]
    ids = jnp.broadcast_to(request.astype(F32), (8, ATOM_DEV))
    slot_atom = mm_nt(ids.astype(BF16), spread_atom.astype(BF16))[0:1]
    lane_block = lax.broadcasted_iota(jnp.int32, (1, ROWS), 1) // SLOT_ROWS
    atom_row = lax.broadcasted_iota(jnp.int32, (ATOM_DEV, ROWS), 0).astype(F32)
    for k in range(BLOCKS):
        wanted = jnp.where(lane_block == k, slot_atom, -1.0)
        select[k] = (atom_row == wanted).astype(BF16)
    fsend[...] = jnp.zeros_like(fsend)
    rsum[...] = jnp.zeros_like(rsum)
    own[...] = jnp.zeros_like(own)

    high = high_ref[0]
    inverse = 1.0 / jnp.broadcast_to(high - low_ref[0], (1, ROWS))
    diagonal = (
        lax.broadcasted_iota(jnp.int32, (ROWS, ROWS), 0)
        == lax.broadcasted_iota(jnp.int32, (ROWS, ROWS), 1)
    ).astype(F32) * high

    def step(i):
        taken = branch_ref[i].astype(F32)
        return 2.0 * taken, 1.0 - 2.0 * taken

    def square_block(src, rows, cols, depth):
        lh = xh[src, rows, depth]
        ll = xl[src, rows, depth]
        rh = xh[src, depth, cols]
        rl = xl[src, depth, cols]
        return mm(lh, rh) + mm(ll, rh) + mm(lh, rl)

    def finish(src, dst, i, j, square, scale):
        old = xh[src, span(i), span(j)].astype(F32) + xl[src, span(i), span(j)].astype(F32)
        new = scale[0] * old + scale[1] * square
        h, l = split2(new)
        xh[dst, span(i), span(j)] = h
        xl[dst, span(i), span(j)] = l
        if i < j:
            th, tl = split2(new.T)
            xh[dst, span(j), span(i)] = th
            xl[dst, span(j), span(i)] = tl

    load_core.wait()
    own_part = core[:, 0:ROWS]
    start = (diagonal - 0.5 * (own_part + own_part.T)) * inverse
    h, l = split2(start)
    xh[0, 0:ROWS, 0:ROWS] = h
    xl[0, 0:ROWS, 0:ROWS] = l
    cross = -(core[:, ROWS:M] * live_row) * inverse
    h, l = split2(cross)
    xh[0, 0:ROWS, ROWS:M] = h
    xl[0, 0:ROWS, ROWS:M] = l
    h, l = split2(cross.T)
    xh[0, ROWS:M, 0:ROWS] = h
    xl[0, ROWS:M, 0:ROWS] = l
    scale = step(0)
    for j in range(COLS):
        for i in range(j + 1):
            if j < 2:
                finish(0, 1, i, j, square_block(0, span(i), span(j), slice(0, M)), scale)
            elif i < 2:
                acc[span(i), span(j)] = square_block(0, span(i), span(j), slice(0, ROWS))

    for send in sends:
        send.wait()
    received = halo[...]
    start = (diagonal * live_col - 0.5 * (received + received.T) * live_col * live_row) * inverse
    h, l = split2(start)
    xh[0, ROWS:M, ROWS:M] = h
    xl[0, ROWS:M, ROWS:M] = l
    for j in range(2, COLS):
        for i in range(j + 1):
            if i < 2:
                part = acc[span(i), span(j)] + square_block(0, span(i), span(j), slice(ROWS, M))
            else:
                part = square_block(0, span(i), span(j), slice(0, M))
            finish(0, 1, i, j, part, scale)

    def middle(number, carry):
        src = lax.rem(number, 2)
        dst = 1 - src
        weights = step(number)
        for j in range(COLS):
            for i in range(j + 1):
                finish(src, dst, i, j, square_block(src, span(i), span(j), slice(0, M)), weights)
        return carry

    lax.fori_loop(1, ITERS - 1, middle, 0)

    last = (ITERS - 1) % 2
    scale = step(ITERS - 1)
    for load in load_deriv:
        load.wait()
    zero = jnp.zeros((8, 128), F32)
    writes = []

    def column(q):
        old = xh[last, 0:ROWS, span(q)].astype(F32) + xl[last, 0:ROWS, span(q)].astype(F32)
        square = square_block(last, slice(0, ROWS), span(q), slice(0, M))
        new = scale[0] * old + scale[1] * square
        for side in range(2):
            tile = 2 * q + side
            lanes = slice(tile * 128, (tile + 1) * 128)
            dens[tile] = new[:, side * 128 : (side + 1) * 128]
            write = pltpu.make_async_copy(dens.at[tile], dens_ref.at[:, lanes], dens_sem.at[tile])
            write.start()
            writes.append(write)

        def group(g, sums):
            sums = [list(pair) for pair in sums]
            atoms = pl.ds(pl.multiple_of(g * 8, 8), 8)
            local = [None, None, None]
            for side in range(2):
                lanes = slice(q * TILE + side * 128, q * TILE + (side + 1) * 128)
                rows = [dens[2 * q + side, pl.ds(g * 8 * ORB + mu, 8, stride=ORB)] for mu in range(ORB)]
                for c in range(3):
                    term = rows[0] * dbuf[c, 0, atoms, lanes]
                    for mu in range(1, ORB):
                        term = term + rows[mu] * dbuf[c, mu, atoms, lanes]
                    sums[c][side] = sums[c][side] + term
                    local[c] = term if side == 0 else local[c] + term
            for c in range(3):
                own[c, atoms] += local[c]
            return tuple(tuple(pair) for pair in sums)

        sums = lax.fori_loop(0, ATOM_DEV // 8, group, ((zero, zero),) * 3, unroll=4)
        return [[jnp.sum(value, axis=0, keepdims=True) for value in pair] for pair in sums]

    def by_parts(sums):
        for c in range(3):
            rsum[c : c + 1] = jnp.concatenate([piece[c] for piece in sums], axis=1)
        parts = split3(rsum[0:8])
        return jnp.concatenate([p.astype(F32) for p in parts], axis=0).astype(BF16)

    def joined(value):
        return value[0:8] + value[8:16] + value[16:24]

    def halves(triples, which):
        return [t[which] for t in triples]

    two = column(2)
    three = column(3)
    four = column(4)
    halo_sums = by_parts([halves(two, 1), halves(three, 0), halves(three, 1), halves(four, 0), halves(four, 1)])
    exchanges = []
    for k in range(BLOCKS):
        terms = -2.0 * joined(mm_nt(halo_sums, select[k]))
        fsend[k, :, 0:ATOM_DEV] = terms
        send = pltpu.make_async_remote_copy(
            src_ref=fsend.at[k],
            dst_ref=frecv.at[k],
            send_sem=fsend_sem.at[k],
            recv_sem=frecv_sem.at[k],
            device_id=(peer(block_offset(k)),),
            device_id_type=MESH,
        )
        send.start()
        exchanges.append(send)
    zeroth = column(0)
    first = column(1)
    core_sums = by_parts([halves(zeroth, 0), halves(zeroth, 1), halves(first, 0), halves(first, 1), halves(two, 0)])
    atom_of_lane = (
        lax.broadcasted_iota(jnp.int32, (ATOM_DEV, ROWS), 1) // ORB
        == lax.broadcasted_iota(jnp.int32, (ATOM_DEV, ROWS), 0)
    ).astype(BF16)
    total = -2.0 * joined(mm_nt(core_sums, atom_of_lane))
    ones = jnp.ones((8, 3 * 128), BF16)
    row_of = lax.broadcasted_iota(jnp.int32, (8, ATOM_DEV), 0)
    for c in range(3):
        parts = jnp.concatenate([p.astype(F32) for p in split3(own[c])], axis=1).astype(BF16)
        total = total + jnp.where(row_of == c, 2.0 * mm_nt(ones, parts), 0.0)
    for exchange in exchanges:
        exchange.wait()
    for k in range(BLOCKS):
        total = total + frecv[k, :, 0:ATOM_DEV]
    force_ref[...] = total[0:3]
    for write in writes:
        write.wait()


def per_device(ham_core, halo_rows, halo_request, deriv, e_low, e_high, branches):
    smem = pl.BlockSpec(memory_space=pltpu.SMEM)
    vmem = pl.BlockSpec(memory_space=pltpu.VMEM)
    hbm = pl.BlockSpec(memory_space=pl.ANY)
    dma = pltpu.SemaphoreType.DMA
    return pl.pallas_call(
        sp2_kernel,
        out_shape=(
            jax.ShapeDtypeStruct((ROWS, M), F32),
            jax.ShapeDtypeStruct((3, ATOM_DEV), F32),
        ),
        in_specs=[smem, smem, smem, vmem, hbm, hbm, hbm],
        out_specs=(hbm, vmem),
        scratch_shapes=[
            pltpu.VMEM((ROWS, M), F32),
            pltpu.VMEM((ROWS, ROWS), F32),
            pltpu.VMEM((3, ORB, ATOM_DEV, M), F32),
            pltpu.VMEM((2, M, M), BF16),
            pltpu.VMEM((2, M, M), BF16),
            pltpu.VMEM((2 * TILE, M), F32),
            pltpu.VMEM((2 * COLS, ROWS, 128), F32),
            pltpu.VMEM((3, ATOM_DEV, 128), F32),
            pltpu.VMEM((BLOCKS, ATOM_DEV, ROWS), BF16),
            pltpu.VMEM((8, ROWS), F32),
            pltpu.VMEM((BLOCKS, 8, TILE), F32),
            pltpu.VMEM((BLOCKS, 8, TILE), F32),
            dma((1,)),
            dma((3 * ORB,)),
            dma((2 * COLS,)),
            dma((BLOCKS,)),
            dma((BLOCKS,)),
            dma((BLOCKS,)),
            dma((BLOCKS,)),
        ],
        compiler_params=pltpu.CompilerParams(
            collective_id=0, has_side_effects=True, vmem_limit_bytes=60 << 20
        ),
    )(e_low, e_high, branches, halo_request, ham_core, halo_rows, deriv)


def solution(mesh):
    in_specs = (
        P("dom", None),
        P("dom", None, None, None),
        P("dom", None),
        P(None, "dom", None, None),
        P(),
        P(),
        P(),
    )
    out_specs = (P("dom", None), P(None, "dom"))
    return jax.shard_map(
        per_device, mesh=mesh, in_specs=in_specs, out_specs=out_specs, check_vma=False
    )
```

time: 295 us -> 106 us (0.36); the launches traced: 291 us -> 105 us
  matrix products: 150 us -> 0 us
  Pallas kernels: 0 us -> 99 us
  local copies, waits for them, and re-layouts: 45.2 us -> 4.44 us
  starting transfers between devices: 39.6 us -> 0 us
  waiting for transfers between devices: 28.3 us -> 0 us
  other arithmetic: 21.9 us -> 0 us
  between operations: 5.55 us -> 1.94 us
    dot_general x6 -> x0, matrix products: 150 us -> none  [the longest x5 150 us: product(): jnp.dot(left, right, precision=lax.Precision.HIGHEST, preferred_element_t...]
    pallas_call x0 -> x1, Pallas kernels: none -> 99 us  [per_device(): pl.pallas_call(sp2_kernel, out_shape=(jax.ShapeDtypeStruct((ROWS, M), F32...]
    ppermute x16 -> x0, starting transfers between devices: 39.6 us -> none  [passed_along(): return lax.ppermute(value, axis, pairs)]
    ppermute x16 -> x0, waiting for transfers between devices: 28.3 us -> none  [passed_along(): return lax.ppermute(value, axis, pairs)]
    reduce_sum x3 -> x0, other arithmetic: 15.6 us -> none  [the longest x1 10.8 us: per_device(): jnp.sum(density.reshape(ATOM_DEV, ORB, order_all)[None] * deriv, axis=2)]
    mul x2 -> x0, local copies, waits for them, and re-layouts: 10.9 us -> none  [the longest x1 8.17 us: per_device(): jnp.concatenate([ham_core, arrived.reshape(-1, order_all)], axis=0)]
    unnamed x15 -> x4, local copies, waits for them, and re-layouts: 14.5 us -> 4.44 us
    reshape x4 -> x0, local copies, waits for them, and re-layouts: 9.85 us -> none  [the longest x1 5.11 us: per_device(): pair_force = 2.0 * jnp.sum(weighted.reshape(3, ATOM_DEV, -1, ORB), axis=3)]
  transfers between devices with their start and end apart: 16 -> 0, of which waited for: 6 -> 0; matrix products, arithmetic and copies ran while one was open for 6% -> 0% of each run, Pallas kernels for 0% -> 0%
where the time goes in v1:
time: 106 us; the launch traced here: 105 us
  Pallas kernels  99 us (93%)
  local copies, waits for them, and re-layouts  4.44 us (4%)
  between operations  1.94 us (2%)
    pallas_call x1, Pallas kernels, per_device(): pl.pallas_call(sp2_kernel, out_shape=(jax.ShapeDtypeStruct((ROWS, M), F32...  99 us
    unnamed x4, local copies, waits for them, and re-layouts  4.44 us

profile of v1, /device:TPU:1, one launch (start us, length us, event | category | flops | bytes accessed | tf_op | source)
XLA Modules:
  0.0 105.4 jit_solution(7213226694761193337)
XLA Ops:
  1.9 99.0 %shard_map.86 = (f32[640,1280]{1,0:T(8,128)}, f32[3,160]{1,0:T(4,128)}) custom-call(f32[1]{0:T(128)S(6)} %copy.11.low_ref, f32[1]{0:T(128)S(6)} %copy.12.high_ref, s32[5]{0:T(128)} %branch_ref.1, s32[1,160]{1,0:T(1,128)} %request_ref.1, f32[640,1280]{1,0:T(8,128)} %ham_ref.1, f32[1,8,80,1280]{3,2,1,0:T(8,128)} %halo_ref.1, f32[3,160,4,1280]{3,2,1,0:T(4,128)} %deriv_ref.1), custom_call_target="tpu_custom_call" | custom-call | tf_op jit(solution)/shard_map/pallas_call | solution.py:282
  100.9 0.0 copy-start
  100.9 3.8 %copy.13 = f32[640,1280]{1,0:T(8,128)} copy(f32[640,1280]{1,0:T(8,128)} %get-tuple-element.4) | data formatting | bytes 6553600
  104.8 0.0 copy-done
  104.8 0.6 copy.14
Async XLA Ops:
  100.9 3.9 %copy-start = (f32[3,160]{1,0:T(4,128)S(1)}, f32[3,160]{1,0:T(4,128)}, u32[]{:S(2)}) copy-start(f32[3,160]{1,0:T(4,128)} %get-tuple-element.5) | copy-start | bytes 5764

commit v2 on v1

--- a/solution.py
+++ b/solution.py
@@ -53,8 +53,8 @@
 def sp2_kernel(
     low_ref, high_ref, branch_ref, request_ref, ham_ref, halo_ref, deriv_ref,
     dens_ref, force_ref,
-    core, halo, dbuf, xh, xl, acc, dens, own, select, rsum, fsend, frecv,
-    core_sem, deriv_sem, dens_sem, send_sem, recv_sem, fsend_sem, frecv_sem,
+    core, halo, dbuf, even_h, even_l, odd_h, odd_l, acc, dens, own, select, rsum, fsend, frecv,
+    core_sem, deriv_sem, send_sem, recv_sem, fsend_sem, frecv_sem,
 ):
     count = lax.axis_size("dom")
     me = lax.axis_index("dom")
@@ -118,37 +118,36 @@
         taken = branch_ref[i].astype(F32)
         return 2.0 * taken, 1.0 - 2.0 * taken
 
+    pairs = ((even_h, even_l), (odd_h, odd_l))
+    first_h, first_l = pairs[0]
+
     def square_block(src, rows, cols, depth):
-        lh = xh[src, rows, depth]
-        ll = xl[src, rows, depth]
-        rh = xh[src, depth, cols]
-        rl = xl[src, depth, cols]
-        return mm(lh, rh) + mm(ll, rh) + mm(lh, rl)
+        xh, xl = pairs[src]
+        rh = xh[depth, cols]
+        return mm(xh[rows, depth], rh) + mm(xl[rows, depth], rh) + mm(xh[rows, depth], xl[depth, cols])
 
     def finish(src, dst, i, j, square, scale):
-        old = xh[src, span(i), span(j)].astype(F32) + xl[src, span(i), span(j)].astype(F32)
+        xh, xl = pairs[src]
+        yh, yl = pairs[dst]
+        old = xh[span(i), span(j)].astype(F32) + xl[span(i), span(j)].astype(F32)
         new = scale[0] * old + scale[1] * square
-        h, l = split2(new)
-        xh[dst, span(i), span(j)] = h
-        xl[dst, span(i), span(j)] = l
+        yh[span(i), span(j)], yl[span(i), span(j)] = split2(new)
         if i < j:
-            th, tl = split2(new.T)
-            xh[dst, span(j), span(i)] = th
-            xl[dst, span(j), span(i)] = tl
+            yh[span(j), span(i)], yl[span(j), span(i)] = split2(new.T)
 
     load_core.wait()
     own_part = core[:, 0:ROWS]
     start = (diagonal - 0.5 * (own_part + own_part.T)) * inverse
     h, l = split2(start)
-    xh[0, 0:ROWS, 0:ROWS] = h
-    xl[0, 0:ROWS, 0:ROWS] = l
+    first_h[0:ROWS, 0:ROWS] = h
+    first_l[0:ROWS, 0:ROWS] = l
     cross = -(core[:, ROWS:M] * live_row) * inverse
     h, l = split2(cross)
-    xh[0, 0:ROWS, ROWS:M] = h
-    xl[0, 0:ROWS, ROWS:M] = l
+    first_h[0:ROWS, ROWS:M] = h
+    first_l[0:ROWS, ROWS:M] = l
     h, l = split2(cross.T)
-    xh[0, ROWS:M, 0:ROWS] = h
-    xl[0, ROWS:M, 0:ROWS] = l
+    first_h[ROWS:M, 0:ROWS] = h
+    first_l[ROWS:M, 0:ROWS] = l
     scale = step(0)
     for j in range(COLS):
         for i in range(j + 1):
@@ -162,8 +161,8 @@
     received = halo[...]
     start = (diagonal * live_col - 0.5 * (received + received.T) * live_col * live_row) * inverse
     h, l = split2(start)
-    xh[0, ROWS:M, ROWS:M] = h
-    xl[0, ROWS:M, ROWS:M] = l
+    first_h[ROWS:M, ROWS:M] = h
+    first_l[ROWS:M, ROWS:M] = l
     for j in range(2, COLS):
         for i in range(j + 1):
             if i < 2:
@@ -172,39 +171,32 @@
                 part = square_block(0, span(i), span(j), slice(0, M))
             finish(0, 1, i, j, part, scale)
 
-    def middle(number, carry):
-        src = lax.rem(number, 2)
-        dst = 1 - src
+    for number in range(1, ITERS - 1):
+        src = number % 2
         weights = step(number)
         for j in range(COLS):
             for i in range(j + 1):
-                finish(src, dst, i, j, square_block(src, span(i), span(j), slice(0, M)), weights)
-        return carry
-
-    lax.fori_loop(1, ITERS - 1, middle, 0)
+                finish(src, 1 - src, i, j, square_block(src, span(i), span(j), slice(0, M)), weights)
 
     last = (ITERS - 1) % 2
     scale = step(ITERS - 1)
     for load in load_deriv:
         load.wait()
     zero = jnp.zeros((8, 128), F32)
-    writes = []
 
     def column(q):
-        old = xh[last, 0:ROWS, span(q)].astype(F32) + xl[last, 0:ROWS, span(q)].astype(F32)
+        xh, xl = pairs[last]
+        old = xh[0:ROWS, span(q)].astype(F32) + xl[0:ROWS, span(q)].astype(F32)
         square = square_block(last, slice(0, ROWS), span(q), slice(0, M))
         new = scale[0] * old + scale[1] * square
         for side in range(2):
             tile = 2 * q + side
-            lanes = slice(tile * 128, (tile + 1) * 128)
             dens[tile] = new[:, side * 128 : (side + 1) * 128]
-            write = pltpu.make_async_copy(dens.at[tile], dens_ref.at[:, lanes], dens_sem.at[tile])
-            write.start()
-            writes.append(write)
+        dens_ref[:, span(q)] = new
 
         def group(g, sums):
             sums = [list(pair) for pair in sums]
-            atoms = pl.ds(pl.multiple_of(g * 8, 8), 8)
+            atoms = slice(g * 8, g * 8 + 8)
             local = [None, None, None]
             for side in range(2):
                 lanes = slice(q * TILE + side * 128, q * TILE + (side + 1) * 128)
@@ -219,7 +211,9 @@
                 own[c, atoms] += local[c]
             return tuple(tuple(pair) for pair in sums)
 
-        sums = lax.fori_loop(0, ATOM_DEV // 8, group, ((zero, zero),) * 3, unroll=4)
+        sums = ((zero, zero),) * 3
+        for g in range(ATOM_DEV // 8):
+            sums = group(g, sums)
         return [[jnp.sum(value, axis=0, keepdims=True) for value in pair] for pair in sums]
 
     def by_parts(sums):
@@ -270,8 +264,6 @@
     for k in range(BLOCKS):
         total = total + frecv[k, :, 0:ATOM_DEV]
     force_ref[...] = total[0:3]
-    for write in writes:
-        write.wait()
 
 
 def per_device(ham_core, halo_rows, halo_request, deriv, e_low, e_high, branches):
@@ -282,17 +274,19 @@
     return pl.pallas_call(
         sp2_kernel,
         out_shape=(
-            jax.ShapeDtypeStruct((ROWS, M), F32),
-            jax.ShapeDtypeStruct((3, ATOM_DEV), F32),
+            pltpu.VMEM((ROWS, M), F32),
+            pltpu.VMEM((3, ATOM_DEV), F32),
         ),
         in_specs=[smem, smem, smem, vmem, hbm, hbm, hbm],
-        out_specs=(hbm, vmem),
+        out_specs=(vmem, vmem),
         scratch_shapes=[
             pltpu.VMEM((ROWS, M), F32),
             pltpu.VMEM((ROWS, ROWS), F32),
             pltpu.VMEM((3, ORB, ATOM_DEV, M), F32),
-            pltpu.VMEM((2, M, M), BF16),
-            pltpu.VMEM((2, M, M), BF16),
+            pltpu.VMEM((M, M), BF16),
+            pltpu.VMEM((M, M), BF16),
+            pltpu.VMEM((M, M), BF16),
+            pltpu.VMEM((M, M), BF16),
             pltpu.VMEM((2 * TILE, M), F32),
             pltpu.VMEM((2 * COLS, ROWS, 128), F32),
             pltpu.VMEM((3, ATOM_DEV, 128), F32),
@@ -302,14 +296,13 @@
             pltpu.VMEM((BLOCKS, 8, TILE), F32),
             dma((1,)),
             dma((3 * ORB,)),
-            dma((2 * COLS,)),
             dma((BLOCKS,)),
             dma((BLOCKS,)),
             dma((BLOCKS,)),
             dma((BLOCKS,)),
         ],
         compiler_params=pltpu.CompilerParams(
-            collective_id=0, has_side_effects=True, vmem_limit_bytes=60 << 20
+            collective_id=0, has_side_effects=True, vmem_limit_bytes=52 << 20
         ),
     )(e_low, e_high, branches, halo_request, ham_core, halo_rows, deriv)
 

time: 106 us -> 80.3 us (0.76)
  Pallas kernels: 99 us -> 75.9 us
  local copies, waits for them, and re-layouts: 4.44 us -> 2.3 us
    pallas_call x1, Pallas kernels: 99 us -> 75.9 us  [per_device(): pl.pallas_call(sp2_kernel, out_shape=(pltpu.VMEM((ROWS, M), F32), pltpu.V...]
    unnamed x4 -> x2, local copies, waits for them, and re-layouts: 4.44 us -> 2.3 us
where the time goes in v2:
time: 80.3 us; the launch traced here: 80.2 us
  Pallas kernels  75.9 us (95%)
  local copies, waits for them, and re-layouts  2.3 us (3%)
  between operations  1.93 us (2%)
    pallas_call x1, Pallas kernels, per_device(): pl.pallas_call(sp2_kernel, out_shape=(pltpu.VMEM((ROWS, M), F32), pltpu.V...  75.9 us
    unnamed x2, local copies, waits for them, and re-layouts  2.3 us

profile of v2, /device:TPU:1, one launch (start us, length us, event | category | flops | bytes accessed | tf_op | source)
XLA Modules:
  0.0 80.2 jit_solution(8491699297122524380)
XLA Ops:
  1.9 75.9 %shard_map.86 = (f32[640,1280]{1,0:T(8,128)S(1)}, f32[3,160]{1,0:T(4,128)S(1)}) custom-call(f32[1]{0:T(128)S(6)} %copy.13.low_ref, f32[1]{0:T(128)S(6)} %copy.14.high_ref, s32[5]{0:T(128)} %branch_ref.1, s32[1,160]{1,0:T(1,128)} %request_ref.1, f32[640,1280]{1,0:T(8,128)} %ham_ref.1, f32[1,8,80,1280]{3,2,1,0:T(8,128)} %halo_ref.1, f32[3,160,4,1280]{3,2,1,0:T(4,128)} %deriv_ref.1), custom_call_target="tpu_custom_call" | custom-call | tf_op jit(solution)/shard_map/pallas_call | solution.py:274
  77.8 1.7 %copy.11 = f32[640,1280]{1,0:T(8,128)} copy(f32[640,1280]{1,0:T(8,128)S(1)} %get-tuple-element.2) | data formatting | bytes 6553600
  79.6 0.6 copy.12

commit v3 on v2

--- a/solution.py
+++ b/solution.py
@@ -17,6 +17,7 @@
 COLS = M // TILE
 F32 = jnp.float32
 BF16 = jnp.bfloat16
+CUTS = (0, 384, 640)
 MESH = pl.DeviceIdType.MESH
 
 
@@ -68,18 +69,25 @@
     for k in range(BLOCKS):
         pl.semaphore_signal(barrier, inc=1, device_id=(peer(block_offset(k)),), device_id_type=MESH)
     pl.semaphore_wait(barrier, BLOCKS)
-    sends = []
-    for k in (3, 7, 2, 6, 1, 5, 0, 4):
-        send = pltpu.make_async_remote_copy(
-            src_ref=halo_ref.at[0, k, :, ROWS:M],
-            dst_ref=halo.at[k * SLOT_ROWS : (k + 1) * SLOT_ROWS],
-            send_sem=send_sem.at[k],
-            recv_sem=recv_sem.at[k],
+
+    def halo_copy(phase, k):
+        return pltpu.make_async_remote_copy(
+            src_ref=halo_ref.at[0, k, :, ROWS + CUTS[phase] : ROWS + CUTS[phase + 1]],
+            dst_ref=halo.at[k * SLOT_ROWS : (k + 1) * SLOT_ROWS, CUTS[phase] : CUTS[phase + 1]],
+            send_sem=send_sem.at[phase, k],
+            recv_sem=recv_sem.at[phase, k],
             device_id=(peer(-block_offset(k)),),
             device_id_type=MESH,
         )
-        send.start()
-        sends.append(send)
+
+    def send_all(order):
+        for phase in range(2):
+            for k in order:
+                halo_copy(phase, k).start()
+
+    on_first = lax.rem(me, 2) == 0
+    pl.when(on_first)(lambda: send_all((3, 7, 2, 6, 1, 5, 0, 4)))
+    pl.when(jnp.logical_not(on_first))(lambda: send_all((0, 4, 1, 5, 2, 6, 3, 7)))
     load_deriv = []
     for c in range(3):
         for mu in range(ORB):
@@ -123,8 +131,12 @@
 
     def square_block(src, rows, cols, depth):
         xh, xl = pairs[src]
-        rh = xh[depth, cols]
-        return mm(xh[rows, depth], rh) + mm(xl[rows, depth], rh) + mm(xh[rows, depth], xl[depth, cols])
+        left = xh[rows, depth]
+        right = xh[depth, cols]
+        small = mm(left, xl[depth, cols])
+        if rows == cols:
+            return mm(left, right) + (small + small.T)
+        return mm(left, right) + mm(xl[rows, depth], right) + small
 
     def finish(src, dst, i, j, square, scale):
         xh, xl = pairs[src]
@@ -149,27 +161,47 @@
     first_h[ROWS:M, 0:ROWS] = h
     first_l[ROWS:M, 0:ROWS] = l
     scale = step(0)
-    for j in range(COLS):
-        for i in range(j + 1):
-            if j < 2:
-                finish(0, 1, i, j, square_block(0, span(i), span(j), slice(0, M)), scale)
-            elif i < 2:
-                acc[span(i), span(j)] = square_block(0, span(i), span(j), slice(0, ROWS))
-
-    for send in sends:
-        send.wait()
-    received = halo[...]
-    start = (diagonal * live_col - 0.5 * (received + received.T) * live_col * live_row) * inverse
-    h, l = split2(start)
-    first_h[ROWS:M, ROWS:M] = h
-    first_l[ROWS:M, ROWS:M] = l
-    for j in range(2, COLS):
-        for i in range(j + 1):
-            if i < 2:
-                part = acc[span(i), span(j)] + square_block(0, span(i), span(j), slice(ROWS, M))
-            else:
-                part = square_block(0, span(i), span(j), slice(0, M))
-            finish(0, 1, i, j, part, scale)
+    whole = slice(0, M)
+    near = slice(ROWS, ROWS + CUTS[1])
+    far = slice(ROWS + CUTS[1], M)
+    later = [(i, j) for j in range(2, COLS) for i in range(j + 1)]
+
+    def kept(i, j):
+        return span(i), slice(j * TILE - 2 * TILE, (j + 1) * TILE - 2 * TILE)
+
+    for i, j in ((0, 0), (0, 1), (1, 1)):
+        finish(0, 1, i, j, square_block(0, span(i), span(j), whole), scale)
+    for i, j in later:
+        acc[kept(i, j)] = square_block(0, span(i), span(j), slice(0, ROWS))
+
+    def halo_start(rows, cols):
+        both = halo[rows, cols] + halo[cols, rows].T
+        value = -0.5 * both * live_col[rows] * live_row[:, cols]
+        if rows == cols:
+            value = value + diagonal[rows, cols] * live_col[rows]
+        return value * inverse[:, cols]
+
+    def put_start(rows, cols):
+        value = halo_start(rows, cols)
+        there = slice(ROWS + rows.start, ROWS + rows.stop), slice(ROWS + cols.start, ROWS + cols.stop)
+        first_h[there], first_l[there] = split2(value)
+        if rows != cols:
+            first_h[there[1], there[0]], first_l[there[1], there[0]] = split2(value.T)
+
+    early, late = slice(CUTS[0], CUTS[1]), slice(CUTS[1], CUTS[2])
+    for k in range(BLOCKS):
+        halo_copy(0, k).wait_recv()
+    put_start(early, early)
+    for i, j in later:
+        if j < COLS - 1:
+            acc[kept(i, j)] += square_block(0, span(i), span(j), near)
+    for k in range(BLOCKS):
+        halo_copy(1, k).wait_recv()
+    put_start(early, late)
+    put_start(late, late)
+    for i, j in later:
+        depth = far if j < COLS - 1 else slice(ROWS, M)
+        finish(0, 1, i, j, acc[kept(i, j)] + square_block(0, span(i), span(j), depth), scale)
 
     for number in range(1, ITERS - 1):
         src = number % 2
@@ -182,18 +214,37 @@
     scale = step(ITERS - 1)
     for load in load_deriv:
         load.wait()
+    for phase in range(2):
+        for k in range(BLOCKS):
+            halo_copy(phase, k).wait_send()
     zero = jnp.zeros((8, 128), F32)
 
-    def column(q):
+    def final_block(rows, cols):
         xh, xl = pairs[last]
-        old = xh[0:ROWS, span(q)].astype(F32) + xl[0:ROWS, span(q)].astype(F32)
-        square = square_block(last, slice(0, ROWS), span(q), slice(0, M))
-        new = scale[0] * old + scale[1] * square
-        for side in range(2):
-            tile = 2 * q + side
-            dens[tile] = new[:, side * 128 : (side + 1) * 128]
-        dens_ref[:, span(q)] = new
-
+        old = xh[rows, cols].astype(F32) + xl[rows, cols].astype(F32)
+        return scale[0] * old + scale[1] * square_block(last, rows, cols, slice(0, M))
+
+    def put_density(row, col, value):
+        height, width = value.shape
+        dens_ref[row : row + height, col : col + width] = value
+        for side in range(width // 128):
+            dens[col // 128 + side, row : row + height] = value[:, side * 128 : (side + 1) * 128]
+
+    def halo_column(q):
+        for row in (0, TILE, 2 * TILE):
+            value = final_block(slice(row, min(row + TILE, ROWS)), span(q))
+            put_density(row, q * TILE, value)
+            if q == 2 and row < 2 * TILE:
+                put_density(2 * TILE, row, value[:, 0 : ROWS - 2 * TILE].T)
+
+    def core_column(q):
+        for i in range(q + 1):
+            value = final_block(span(i), span(q))
+            put_density(i * TILE, q * TILE, value)
+            if i < q:
+                put_density(q * TILE, i * TILE, value.T)
+
+    def force_column(q):
         def group(g, sums):
             sums = [list(pair) for pair in sums]
             atoms = slice(g * 8, g * 8 + 8)
@@ -228,9 +279,13 @@
     def halves(triples, which):
         return [t[which] for t in triples]
 
-    two = column(2)
-    three = column(3)
-    four = column(4)
+    halo_column(2)
+    halo_column(3)
+    two = force_column(2)
+    halo_column(4)
+    three = force_column(3)
+    core_column(0)
+    four = force_column(4)
     halo_sums = by_parts([halves(two, 1), halves(three, 0), halves(three, 1), halves(four, 0), halves(four, 1)])
     exchanges = []
     for k in range(BLOCKS):
@@ -246,8 +301,9 @@
         )
         send.start()
         exchanges.append(send)
-    zeroth = column(0)
-    first = column(1)
+    core_column(1)
+    zeroth = force_column(0)
+    first = force_column(1)
     core_sums = by_parts([halves(zeroth, 0), halves(zeroth, 1), halves(first, 0), halves(first, 1), halves(two, 0)])
     atom_of_lane = (
         lax.broadcasted_iota(jnp.int32, (ATOM_DEV, ROWS), 1) // ORB
@@ -287,7 +343,7 @@
             pltpu.VMEM((M, M), BF16),
             pltpu.VMEM((M, M), BF16),
             pltpu.VMEM((M, M), BF16),
-            pltpu.VMEM((2 * TILE, M), F32),
+            pltpu.VMEM((M, M - 2 * TILE), F32),
             pltpu.VMEM((2 * COLS, ROWS, 128), F32),
             pltpu.VMEM((3, ATOM_DEV, 128), F32),
             pltpu.VMEM((BLOCKS, ATOM_DEV, ROWS), BF16),
@@ -296,8 +352,8 @@
             pltpu.VMEM((BLOCKS, 8, TILE), F32),
             dma((1,)),
             dma((3 * ORB,)),
-            dma((BLOCKS,)),
-            dma((BLOCKS,)),
+            dma((2, BLOCKS)),
+            dma((2, BLOCKS)),
             dma((BLOCKS,)),
             dma((BLOCKS,)),
         ],

time: 80.3 us -> 76 us (0.946)
  Pallas kernels: 75.9 us -> 71.6 us
    pallas_call x1, Pallas kernels: 75.9 us -> 71.6 us  [per_device(): pl.pallas_call(sp2_kernel, out_shape=(pltpu.VMEM((ROWS, M), F32), pltpu.V...]
where the time goes in v3:
time: 76 us; the launch traced here: 75.8 us
  Pallas kernels  71.6 us (94%)
  local copies, waits for them, and re-layouts  2.3 us (3%)
  between operations  1.93 us (3%)
    pallas_call x1, Pallas kernels, per_device(): pl.pallas_call(sp2_kernel, out_shape=(pltpu.VMEM((ROWS, M), F32), pltpu.V...  71.6 us
    unnamed x2, local copies, waits for them, and re-layouts  2.3 us

profile of v3, /device:TPU:1, one launch (start us, length us, event | category | flops | bytes accessed | tf_op | source)
XLA Modules:
  0.0 75.8 jit_solution(2193169707371732203)
XLA Ops:
  1.9 71.6 %shard_map.86 = (f32[640,1280]{1,0:T(8,128)S(1)}, f32[3,160]{1,0:T(4,128)S(1)}) custom-call(f32[1]{0:T(128)S(6)} %copy.13.low_ref, f32[1]{0:T(128)S(6)} %copy.14.high_ref, s32[5]{0:T(128)} %branch_ref.1, s32[1,160]{1,0:T(1,128)} %request_ref.1, f32[640,1280]{1,0:T(8,128)} %ham_ref.1, f32[1,8,80,1280]{3,2,1,0:T(8,128)} %halo_ref.1, f32[3,160,4,1280]{3,2,1,0:T(4,128)} %deriv_ref.1), custom_call_target="tpu_custom_call" | custom-call | tf_op jit(solution)/shard_map/pallas_call | solution.py:330
  73.5 1.7 %copy.11 = f32[640,1280]{1,0:T(8,128)} copy(f32[640,1280]{1,0:T(8,128)S(1)} %get-tuple-element.2) | data formatting | bytes 6553600
  75.2 0.6 copy.12

commit v4 on v3

--- a/solution.py
+++ b/solution.py
@@ -80,21 +80,17 @@
             device_id_type=MESH,
         )
 
-    def send_all(order):
-        for phase in range(2):
+    on_first = lax.rem(me, 2) == 0
+
+    def send_phase(phase):
+        def start(order):
             for k in order:
                 halo_copy(phase, k).start()
 
-    on_first = lax.rem(me, 2) == 0
-    pl.when(on_first)(lambda: send_all((3, 7, 2, 6, 1, 5, 0, 4)))
-    pl.when(jnp.logical_not(on_first))(lambda: send_all((0, 4, 1, 5, 2, 6, 3, 7)))
-    load_deriv = []
-    for c in range(3):
-        for mu in range(ORB):
-            load = pltpu.make_async_copy(deriv_ref.at[c, :, mu, :], dbuf.at[c, mu], deriv_sem.at[c * ORB + mu])
-            load.start()
-            load_deriv.append(load)
-
+        pl.when(on_first)(lambda: start((3, 7, 2, 6, 1, 5, 0, 4)))
+        pl.when(jnp.logical_not(on_first))(lambda: start((0, 4, 1, 5, 2, 6, 3, 7)))
+
+    send_phase(0)
     request = request_ref[...]
     live = (request >= 0).astype(F32)
     spread_atom = (
@@ -188,6 +184,7 @@
         if rows != cols:
             first_h[there[1], there[0]], first_l[there[1], there[0]] = split2(value.T)
 
+    send_phase(1)
     early, late = slice(CUTS[0], CUTS[1]), slice(CUTS[1], CUTS[2])
     for k in range(BLOCKS):
         halo_copy(0, k).wait_recv()
@@ -197,6 +194,13 @@
             acc[kept(i, j)] += square_block(0, span(i), span(j), near)
     for k in range(BLOCKS):
         halo_copy(1, k).wait_recv()
+    load_deriv = []
+    for c in range(3):
+        for mu in range(ORB):
+            load = pltpu.make_async_copy(deriv_ref.at[c, :, mu, :], dbuf.at[c, mu], deriv_sem.at[c * ORB + mu])
+            load.start()
+            load_deriv.append(load)
+
     put_start(early, late)
     put_start(late, late)
     for i, j in later:

time: 76 us -> 77 us (1.013)
  Pallas kernels: 71.6 us -> 72.7 us
    pallas_call x1, Pallas kernels: 71.6 us -> 72.7 us  [per_device(): pl.pallas_call(sp2_kernel, out_shape=(pltpu.VMEM((ROWS, M), F32), pltpu.V...]
where the time goes in v4:
time: 77 us; the launch traced here: 76.9 us
  Pallas kernels  72.7 us (94%)
  local copies, waits for them, and re-layouts  2.3 us (3%)
  between operations  1.93 us (3%)
    pallas_call x1, Pallas kernels, per_device(): pl.pallas_call(sp2_kernel, out_shape=(pltpu.VMEM((ROWS, M), F32), pltpu.V...  72.7 us
    unnamed x2, local copies, waits for them, and re-layouts  2.3 us

profile of v4, /device:TPU:1, one launch (start us, length us, event | category | flops | bytes accessed | tf_op | source)
XLA Modules:
  0.0 76.9 jit_solution(14356038878820715378)
XLA Ops:
  1.9 72.7 %shard_map.86 = (f32[640,1280]{1,0:T(8,128)S(1)}, f32[3,160]{1,0:T(4,128)S(1)}) custom-call(f32[1]{0:T(128)S(6)} %copy.13.low_ref, f32[1]{0:T(128)S(6)} %copy.14.high_ref, s32[5]{0:T(128)} %branch_ref.1, s32[1,160]{1,0:T(1,128)} %request_ref.1, f32[640,1280]{1,0:T(8,128)} %ham_ref.1, f32[1,8,80,1280]{3,2,1,0:T(8,128)} %halo_ref.1, f32[3,160,4,1280]{3,2,1,0:T(4,128)} %deriv_ref.1), custom_call_target="tpu_custom_call" | custom-call | tf_op jit(solution)/shard_map/pallas_call | solution.py:334
  74.6 1.7 %copy.11 = f32[640,1280]{1,0:T(8,128)} copy(f32[640,1280]{1,0:T(8,128)S(1)} %get-tuple-element.2) | data formatting | bytes 6553600
  76.3 0.6 copy.12

commit v5 on v4

--- a/solution.py
+++ b/solution.py
@@ -80,17 +80,17 @@
             device_id_type=MESH,
         )
 
-    on_first = lax.rem(me, 2) == 0
-
-    def send_phase(phase):
-        def start(order):
-            for k in order:
-                halo_copy(phase, k).start()
-
-        pl.when(on_first)(lambda: start((3, 7, 2, 6, 1, 5, 0, 4)))
-        pl.when(jnp.logical_not(on_first))(lambda: start((0, 4, 1, 5, 2, 6, 3, 7)))
-
-    send_phase(0)
+    def start_halo(phase, blocks):
+        for k in blocks:
+            halo_copy(phase, k).start()
+
+    def sent_halo(phase, blocks):
+        for k in blocks:
+            halo_copy(phase, k).wait_send()
+
+    distant, close = (3, 7, 2, 6), (1, 5, 0, 4)
+    start_halo(0, distant)
+
     request = request_ref[...]
     live = (request >= 0).astype(F32)
     spread_atom = (
@@ -184,7 +184,9 @@
         if rows != cols:
             first_h[there[1], there[0]], first_l[there[1], there[0]] = split2(value.T)
 
-    send_phase(1)
+    sent_halo(0, distant)
+    start_halo(0, close)
+    start_halo(1, distant)
     early, late = slice(CUTS[0], CUTS[1]), slice(CUTS[1], CUTS[2])
     for k in range(BLOCKS):
         halo_copy(0, k).wait_recv()
@@ -192,6 +194,8 @@
     for i, j in later:
         if j < COLS - 1:
             acc[kept(i, j)] += square_block(0, span(i), span(j), near)
+    sent_halo(1, distant)
+    start_halo(1, close)
     for k in range(BLOCKS):
         halo_copy(1, k).wait_recv()
     load_deriv = []
@@ -218,9 +222,8 @@
     scale = step(ITERS - 1)
     for load in load_deriv:
         load.wait()
-    for phase in range(2):
-        for k in range(BLOCKS):
-            halo_copy(phase, k).wait_send()
+    sent_halo(0, close)
+    sent_halo(1, close)
     zero = jnp.zeros((8, 128), F32)
 
     def final_block(rows, cols):
@@ -288,7 +291,6 @@
     two = force_column(2)
     halo_column(4)
     three = force_column(3)
-    core_column(0)
     four = force_column(4)
     halo_sums = by_parts([halves(two, 1), halves(three, 0), halves(three, 1), halves(four, 0), halves(four, 1)])
     exchanges = []
@@ -305,6 +307,7 @@
         )
         send.start()
         exchanges.append(send)
+    core_column(0)
     core_column(1)
     zeroth = force_column(0)
     first = force_column(1)

time: 77 us -> 77.7 us (level); the launches traced: 76.9 us -> 76.5 us
  no operation moved by 1% of the time
where the time goes in v5:
time: 77.7 us; the launch traced here: 76.5 us
  Pallas kernels  72.3 us (93%)
  local copies, waits for them, and re-layouts  2.3 us (3%)
  between operations  1.93 us (2%)
    pallas_call x1, Pallas kernels, per_device(): pl.pallas_call(sp2_kernel, out_shape=(pltpu.VMEM((ROWS, M), F32), pltpu.V...  72.3 us
    unnamed x2, local copies, waits for them, and re-layouts  2.3 us

profile of v5, /device:TPU:1, one launch (start us, length us, event | category | flops | bytes accessed | tf_op | source)
XLA Modules:
  0.0 76.5 jit_solution(4507713670284220872)
XLA Ops:
  1.9 72.3 %shard_map.86 = (f32[640,1280]{1,0:T(8,128)S(1)}, f32[3,160]{1,0:T(4,128)S(1)}) custom-call(f32[1]{0:T(128)S(6)} %copy.13.low_ref, f32[1]{0:T(128)S(6)} %copy.14.high_ref, s32[5]{0:T(128)} %branch_ref.1, s32[1,160]{1,0:T(1,128)} %request_ref.1, f32[640,1280]{1,0:T(8,128)} %ham_ref.1, f32[1,8,80,1280]{3,2,1,0:T(8,128)} %halo_ref.1, f32[3,160,4,1280]{3,2,1,0:T(4,128)} %deriv_ref.1), custom_call_target="tpu_custom_call" | custom-call | tf_op jit(solution)/shard_map/pallas_call | solution.py:337
  74.2 1.7 %copy.11 = f32[640,1280]{1,0:T(8,128)} copy(f32[640,1280]{1,0:T(8,128)S(1)} %get-tuple-element.2) | data formatting | bytes 6553600
  75.9 0.6 copy.12

commit v6 on v5

--- a/solution.py
+++ b/solution.py
@@ -167,6 +167,9 @@
 
     for i, j in ((0, 0), (0, 1), (1, 1)):
         finish(0, 1, i, j, square_block(0, span(i), span(j), whole), scale)
+    sent_halo(0, distant)
+    start_halo(0, close)
+    start_halo(1, distant)
     for i, j in later:
         acc[kept(i, j)] = square_block(0, span(i), span(j), slice(0, ROWS))
 
@@ -184,18 +187,15 @@
         if rows != cols:
             first_h[there[1], there[0]], first_l[there[1], there[0]] = split2(value.T)
 
-    sent_halo(0, distant)
-    start_halo(0, close)
-    start_halo(1, distant)
     early, late = slice(CUTS[0], CUTS[1]), slice(CUTS[1], CUTS[2])
     for k in range(BLOCKS):
         halo_copy(0, k).wait_recv()
+    sent_halo(1, distant)
+    start_halo(1, close)
     put_start(early, early)
     for i, j in later:
         if j < COLS - 1:
             acc[kept(i, j)] += square_block(0, span(i), span(j), near)
-    sent_halo(1, distant)
-    start_halo(1, close)
     for k in range(BLOCKS):
         halo_copy(1, k).wait_recv()
     load_deriv = []

time: 77.7 us -> 76 us (0.978)
  Pallas kernels: 72.3 us -> 70.7 us
    pallas_call x1, Pallas kernels: 72.3 us -> 70.7 us  [per_device(): pl.pallas_call(sp2_kernel, out_shape=(pltpu.VMEM((ROWS, M), F32), pltpu.V...]
where the time goes in v6:
time: 76 us; the launch traced here: 74.9 us
  Pallas kernels  70.7 us (93%)
  local copies, waits for them, and re-layouts  2.3 us (3%)
  between operations  1.93 us (3%)
    pallas_call x1, Pallas kernels, per_device(): pl.pallas_call(sp2_kernel, out_shape=(pltpu.VMEM((ROWS, M), F32), pltpu.V...  70.7 us
    unnamed x2, local copies, waits for them, and re-layouts  2.3 us

profile of v6, /device:TPU:1, one launch (start us, length us, event | category | flops | bytes accessed | tf_op | source)
XLA Modules:
  0.0 74.9 jit_solution(11952598767734240085)
XLA Ops:
  1.9 70.7 %shard_map.86 = (f32[640,1280]{1,0:T(8,128)S(1)}, f32[3,160]{1,0:T(4,128)S(1)}) custom-call(f32[1]{0:T(128)S(6)} %copy.13.low_ref, f32[1]{0:T(128)S(6)} %copy.14.high_ref, s32[5]{0:T(128)} %branch_ref.1, s32[1,160]{1,0:T(1,128)} %request_ref.1, f32[640,1280]{1,0:T(8,128)} %ham_ref.1, f32[1,8,80,1280]{3,2,1,0:T(8,128)} %halo_ref.1, f32[3,160,4,1280]{3,2,1,0:T(4,128)} %deriv_ref.1), custom_call_target="tpu_custom_call" | custom-call | tf_op jit(solution)/shard_map/pallas_call | solution.py:337
  72.6 1.7 %copy.11 = f32[640,1280]{1,0:T(8,128)} copy(f32[640,1280]{1,0:T(8,128)S(1)} %get-tuple-element.2) | data formatting | bytes 6553600
  74.3 0.6 copy.12
